TPU v7x, 32 devices: a whole 2x2x4 slice. The times are simulated.
32 devices in a mesh: grp: 2 (over y), scen: 4 (over z), blk: 2 (over x), sub: 2 (over core).
Axes of the slice: x: 2, y: 2, z: 4, core: 2. Of those that a mesh axis runs over, the one named last changes fastest.
Arguments:
- block_matrices: float32 [8, 256, 128, 128], P(('grp', 'scen'), ('blk', 'sub')), parts along dimension 0, may hold values from -0.25 to 0.25
- slot_row_block: int32 [8, 256], P(('grp', 'scen'), ('blk', 'sub')), parts along dimension 0, may hold values from 0 to 7
- tile_column: int32 [8, 256], P(('grp', 'scen'), ('blk', 'sub')), parts along dimension 0, may hold values from 0 to 4127, as said below
- block_count: int32 [8, 4], P(('grp', 'scen'), ('blk', 'sub')), parts along dimension 0, may hold values from 8 to 64, as said below
- carbon_scenario: int32 [8], P(('grp', 'scen')), parts along dimension 0, may hold values from 0 to 23
- intensity: float32 [24, 32, 128], P(None, ('blk', 'sub')), may hold values from 0.2 to 2
- cost_first: float32 [8192, 128], P(('grp', 'scen', 'blk', 'sub')), parts along dimension 0, may hold values from -6 to 6
- lower_first: float32 [8192, 128], P(('grp', 'scen', 'blk', 'sub')), parts along dimension 0, may hold values from -1 to -0.2
- upper_first: float32 [8192, 128], P(('grp', 'scen', 'blk', 'sub')), parts along dimension 0, may hold values from 0.2 to 1
- cost_second: float32 [8, 32, 128], P(('grp', 'scen'), ('blk', 'sub')), parts along dimension 0, may hold values from -6 to 6
- upper_second: float32 [8, 32, 128], P(('grp', 'scen'), ('blk', 'sub')), parts along dimension 0, may hold values from 0.2 to 2
- row_bound: float32 [8, 32, 128], P(('grp', 'scen'), ('blk', 'sub')), parts along dimension 0, may hold values from -20 to 20
- first_start: float32 [8192, 128], P(('grp', 'scen', 'blk', 'sub')), parts along dimension 0, may hold values from -0.2 to 0.2
- second_start: float32 [8, 32, 128], P(('grp', 'scen'), ('blk', 'sub')), parts along dimension 0, may hold values from 0 to 0.2
- dual_start: float32 [8, 32, 128], P(('grp', 'scen'), ('blk', 'sub')), parts along dimension 0, may hold values from 0 to 1
Outputs:
- first_final: float32 [8192, 128], P(('grp', 'scen', 'blk', 'sub')), parts along dimension 0
- second_final: float32 [8, 32, 128], P(('grp', 'scen'), ('blk', 'sub')), parts along dimension 0
- dual_final: float32 [8, 32, 128], P(('grp', 'scen'), ('blk', 'sub')), parts along dimension 0
- residual_norm: float32 [6], P('grp'), parts along dimension 0
There are 2 independent parts, one for each index of `grp`. A program takes and returns all parts, laid end to end along the dimension named above; an argument that names none is the same for every part. Nothing has to cross between parts.
Inputs may be any that keep to these rules, and one draw needn't show every extreme that they name: `block_count`: each scenario has one index of blk and sub with all 64 slots used; the others use between 8 and 32. `tile_column`: values below 4096 name first-section column blocks, values from 4096 on second-section ones. Split the first-section blocks into 16 equal shards in order, and take the slots of one index of scen and of blk and sub together (64 of them, scenario by scenario). In every draw, on every such device, at most 4 of them name first-section blocks of one shard, and some shard is named by exactly 4.
All inputs are finite; a program needn't handle non-finite values.
Results may differ from a plain program's by a relative error of at most 0.0003.
Values sent between devices are 32-bit elements; how exact they have to be, the bound alone decides.
No kernel may reach another device: no remote copies, remote signals or barrier semaphores. Data moves between devices by JAX's collectives and lax.ppermute only.
A program may use at most 64 MiB of HBM per device.

v0:
```python
import jax
import jax.numpy as jnp
from jax import lax
from jax.sharding import PartitionSpec as P

ITERS = 3
precise = lax.Precision.HIGHEST
step_primal = 0.4
step_dual = 0.4


def forward_window(
    block_matrices,
    onehot,
    mask,
    tile_column,
    fetch_first,
    count_first,
    second_bar,
    offset,
    window_size,
):
    count_second = second_bar.shape[1]
    is_first = tile_column < count_first
    from_first = fetch_first(tile_column, offset, window_size)
    second_index = jnp.clip(tile_column - count_first, 0, count_second - 1)
    from_second = jax.vmap(lambda table, index: table[index])(second_bar, second_index)
    blocks = jnp.where(is_first[:, :, None], from_first, from_second)
    product = jnp.einsum("skij,skj->ski", block_matrices, blocks, precision=precise)
    product = product * mask[:, :, None]
    return jnp.einsum("skr,ski->sri", onehot, product, precision=precise)


def adjoint_window(
    block_matrices,
    onehot,
    mask,
    tile_column,
    dual,
    collect_first,
    count_first,
    count_second,
    offset,
    window_size,
):
    gathered = jnp.einsum("skr,sri->ski", onehot, dual, precision=precise)
    product = jnp.einsum("skij,ski->skj", block_matrices, gathered, precision=precise)
    product = product * mask[:, :, None]
    is_first = tile_column < count_first
    first_terms = collect_first(product, tile_column, offset, window_size)
    second_index = jnp.where(is_first, count_second, tile_column - count_first)
    scenario_index = lax.broadcasted_iota(jnp.int32, second_index.shape, 0)
    second_terms = (
        jnp.zeros((product.shape[0], count_second, product.shape[2]), jnp.float32)
        .at[scenario_index, second_index]
        .add(product, mode="drop")
    )
    return (first_terms, second_terms)


def shards(
    block_matrices,
    slot_row_block,
    tile_column,
    block_count,
    carbon_scenario,
    intensity,
    cost_first,
    lower_first,
    upper_first,
    cost_second,
    upper_second,
    row_bound,
    first_start,
    second_start,
    dual_start,
):
    scen_local, slots = slot_row_block.shape
    rows_local = row_bound.shape[1]
    tile_size = row_bound.shape[2]
    shard_first = cost_first.shape[0]
    owner_count = lax.axis_size(("scen", "blk", "sub"))
    count_first = shard_first * owner_count
    count_second = cost_second.shape[1] * lax.axis_size(("blk", "sub"))
    total_cells = scen_local * rows_local * tile_size * owner_count
    mask = (jnp.arange(slots, dtype=jnp.int32)[None, :] < block_count).astype(jnp.float32)
    onehot = (
        slot_row_block[:, :, None] == jnp.arange(rows_local, dtype=jnp.int32)[None, None, :]
    ).astype(jnp.float32)
    choose = (
        carbon_scenario[:, None] == jnp.arange(intensity.shape[0], dtype=jnp.int32)[None, :]
    ).astype(jnp.float32)
    cost_total = cost_second + jnp.einsum("sc,cbt->sbt", choose, intensity, precision=precise)
    first_shape = (count_first, tile_size)

    def collect_first(product, column_window, offset, width):
        first_index = jnp.where(column_window < count_first, column_window, count_first).reshape(-1)
        return (
            jnp.zeros(first_shape, jnp.float32)
            .at[first_index]
            .add(product.reshape(-1, tile_size), mode="drop")
        )

    def make_fetch(first_source):

        def fetch_first(column_window, offset, width):
            return first_source[jnp.clip(column_window, 0, count_first - 1)]

        return fetch_first

    cost_all, lower_all, upper_all, first_now = (
        lax.all_gather(cost_first, ("scen", "blk", "sub"), axis=0, tiled=True),
        lax.all_gather(lower_first, ("scen", "blk", "sub"), axis=0, tiled=True),
        lax.all_gather(upper_first, ("scen", "blk", "sub"), axis=0, tiled=True),
        lax.all_gather(first_start, ("scen", "blk", "sub"), axis=0, tiled=True),
    )
    second_now = second_start
    dual = dual_start
    squares = []
    for step_index in range(ITERS):
        grad_first_part, grad_second_part = adjoint_window(
            block_matrices,
            onehot,
            mask,
            tile_column,
            dual,
            collect_first,
            count_first,
            count_second,
            0,
            slots,
        )
        grad_second = lax.psum_scatter(
            grad_second_part, ("blk", "sub"), scatter_dimension=1, tiled=True
        )
        grad_first = lax.psum(grad_first_part, ("scen", "blk", "sub"))
        first_next = jnp.clip(
            first_now - step_primal * (cost_all - grad_first), lower_all, upper_all
        )
        first_source = 2.0 * first_next - first_now
        second_next = jnp.clip(
            second_now - step_primal * (cost_total - grad_second), 0.0, upper_second
        )
        second_bar = lax.all_gather(
            2.0 * second_next - second_now, ("blk", "sub"), axis=1, tiled=True
        )
        residual = row_bound - forward_window(
            block_matrices,
            onehot,
            mask,
            tile_column,
            make_fetch(first_source),
            count_first,
            second_bar,
            0,
            slots,
        )
        local_square = jnp.sum(residual * residual)
        squares.append(lax.psum(local_square, ("scen", "blk", "sub")))
        dual = jnp.maximum(dual + step_dual * residual, 0.0)
        first_now = first_next
        second_now = second_next
    totals = jnp.stack(squares)
    residual_norm = jnp.sqrt(totals / total_cells)
    offset = lax.axis_index(("scen", "blk", "sub")) * shard_first
    first_final = lax.dynamic_slice_in_dim(first_now, offset, shard_first, 0)
    return (first_final, second_now, dual, residual_norm)


def solution(mesh):
    return jax.shard_map(
        shards,
        mesh=mesh,
        in_specs=(
            P(("grp", "scen"), ("blk", "sub"), None, None),
            P(("grp", "scen"), ("blk", "sub")),
            P(("grp", "scen"), ("blk", "sub")),
            P(("grp", "scen"), ("blk", "sub")),
            P(("grp", "scen")),
            P(None, ("blk", "sub"), None),
            P(("grp", "scen", "blk", "sub"), None),
            P(("grp", "scen", "blk", "sub"), None),
            P(("grp", "scen", "blk", "sub"), None),
            P(("grp", "scen"), ("blk", "sub"), None),
            P(("grp", "scen"), ("blk", "sub"), None),
            P(("grp", "scen"), ("blk", "sub"), None),
            P(("grp", "scen", "blk", "sub"), None),
            P(("grp", "scen"), ("blk", "sub"), None),
            P(("grp", "scen"), ("blk", "sub"), None),
        ),
        out_specs=(
            P(("grp", "scen", "blk", "sub"), None),
            P(("grp", "scen"), ("blk", "sub"), None),
            P(("grp", "scen"), ("blk", "sub"), None),
            P("grp"),
        ),
        check_vma=False,
    )
```

profile of v0, /device:TPU:0, one launch (start us, length us, event | category | flops | bytes accessed | tf_op | source)
XLA Modules:
  0.0 587.6 jit_solution(10443737884723280404)
XLA Ops:
  7.9 0.7 fusion.79
  8.5 0.9 fusion.66
  9.5 5.3 fusion.10
  14.8 2.3 scatter_custom_fusion
  17.2 0.7 all-gather.11.cloned.1.call-update
  17.9 0.7 all-gather.5.cloned.1.call-update
  18.7 0.5 all-gather.7.cloned.1.call-update
  19.2 0.5 all-gather.9.cloned.1.call-update
  19.9 0.9 scatter_custom_fusion.1
  21.4 0.6 dynamic-slice
  22.7 13.2 %all-reduce.1 = f32[1,32,128]{2,1,0:T(8,128)S(1)} all-reduce(f32[1,32,128]{2,1,0:T(8,128)S(1)} %bitcast.135), channel_id=2, replica_groups=mesh['grp'=2,'scen'=4,'blk'=2,'sub'=2] {'blk','sub'}, use_global_device_ids=true, to_apply=%region_3.4.clone | all-reduce | flops 4096 | bytes 32768
  36.1 5.2 all_gather.25
  41.3 0.8 gather_fusion.3
  42.1 75.8 %all-reduce.9.cloned.1.call-done = f32[4096,128]{1,0:T(8,128)} async-done(((f32[4096,128]{1,0:T(8,128)}), f32[4096,128]{1,0:T(8,128)}) %all-reduce.9.cloned.1.call-update) | async-done | bytes 2097168 | tf_op jit(solution)/shard_map/psum | solution.py:136
  117.9 43.1 %all-gather.11.cloned.1.call-done = f32[4096,128]{1,0:T(8,128)} async-done(((f32[256,128]{1,0:T(8,128)}), f32[4096,128]{1,0:T(8,128)}) %all-gather.11.cloned.1.call-update) | async-done | bytes 2097168 | tf_op jit(solution)/shard_map/all_gather | solution.py:112
  160.9 42.6 %all-gather.5.cloned.1.call-done = f32[4096,128]{1,0:T(8,128)} async-done(((f32[256,128]{1,0:T(8,128)}), f32[4096,128]{1,0:T(8,128)}) %all-gather.5.cloned.1.call-update) | async-done | bytes 2097168 | tf_op jit(solution)/shard_map/all_gather | solution.py:114
  203.6 42.5 %all-gather.7.cloned.1.call-done = f32[4096,128]{1,0:T(8,128)} async-done(((f32[256,128]{1,0:T(8,128)}), f32[4096,128]{1,0:T(8,128)}) %all-gather.7.cloned.1.call-update) | async-done | bytes 2097168 | tf_op jit(solution)/shard_map/all_gather | solution.py:113
  246.0 42.4 %all-gather.9.cloned.1.call-done = f32[4096,128]{1,0:T(8,128)} async-done(((f32[256,128]{1,0:T(8,128)}), f32[4096,128]{1,0:T(8,128)}) %all-gather.9.cloned.1.call-update) | async-done | bytes 2097168 | tf_op jit(solution)/shard_map/all_gather | solution.py:115
  288.5 5.9 %multiply_subtract_fusion.2 = (f32[4096,128]{1,0:T(8,128)S(1)}, f32[4096,128]{1,0:T(8,128)}) fusion(f32[4096,128]{1,0:T(8,128)} %all-gather.9.cloned.1.call-done, f32[4096,128]{1,0:T(8,128)} %all-gather.5.cloned.1.call-done, f32[4096,128]{1,0:T(8,128)} %all-gather.7.cloned.1.call-done, f32[4096,128]{1,0:T(8,128)} %all-gather.11.cloned.1.call-done, ...), kind=kLoop, calls=%fused_computation.28 | loop fusion | flops 3670016 | bytes 14680064 | tf_op jit(solution)/shard_map/sub | solution.py:140
  294.4 0.6 gather_fusion
  295.1 8.5 %fusion.8 = f32[64,1,128]{2,1,0:T(1,128)S(1)} fusion(f32[64,128,1]{1,2,0:T(1,128)S(1)} %bitcast.130, f32[1,64,128,128]{3,2,1,0:T(8,128)} %param.15), kind=kOutput, calls=%fused_computation.20 | convolution fusion | flops 12582912 | bytes 4259840 | tf_op jit(solution)/shard_map/skij,skj->ski/dot_general | solution.py:29
  303.6 0.3 fusion.14
  304.1 3.7 fusion.6
  307.7 2.3 scatter_custom_fusion.2
  310.1 0.9 scatter_custom_fusion.3
  311.0 10.4 %all-reduce.2 = f32[1,32,128]{2,1,0:T(8,128)S(1)} all-reduce(f32[1,32,128]{2,1,0:T(8,128)S(1)} %bitcast.137), channel_id=3, replica_groups=mesh['grp'=2,'scen'=4,'blk'=2,'sub'=2] {'blk','sub'}, use_global_device_ids=true, to_apply=%region_7.8.clone | all-reduce | flops 4096 | bytes 32768
  321.4 5.4 all_gather.26
  326.7 0.8 gather_fusion.4
  327.5 79.2 %all-reduce.11.cloned.1.call-done = f32[4096,128]{1,0:T(8,128)} async-done(((f32[4096,128]{1,0:T(8,128)}), f32[4096,128]{1,0:T(8,128)}) %all-reduce.11.cloned.1.call-update) | async-done | bytes 2097168 | tf_op jit(solution)/shard_map/psum | solution.py:136
  406.7 6.2 %multiply_subtract_fusion.1 = (f32[4096,128]{1,0:T(8,128)}, f32[4096,128]{1,0:T(8,128)}) fusion(f32[4096,128]{1,0:T(8,128)} %get-tuple-element.19, f32[4096,128]{1,0:T(8,128)} %all-gather.5.cloned.1.call-done, f32[4096,128]{1,0:T(8,128)} %all-gather.7.cloned.1.call-done, f32[4096,128]{1,0:T(8,128)S(1)} %copy-done.3, f32[4096,128]{1,0:T(8,128)} %all-reduce.11.cloned.1.call-done), kind=kLoop, calls=%fused_computation.26 | loop fusion | flops 3670016 | bytes 14680064 | tf_op jit(solution)/shard_map/sub | solution.py:140
  412.9 2.2 gather_fusion.1
  415.2 8.5 %fusion.4 = f32[64,1,128]{2,1,0:T(1,128)S(1)} fusion(f32[64,128,1]{1,2,0:T(1,128)S(1)} %bitcast.131, f32[1,64,128,128]{3,2,1,0:T(8,128)} %param.15), kind=kOutput, calls=%fused_computation.16 | convolution fusion | flops 12582912 | bytes 4259840 | tf_op jit(solution)/shard_map/skij,skj->ski/dot_general | solution.py:29
  423.6 0.3 fusion.13
  424.2 3.7 fusion.2
  427.8 2.3 scatter_custom_fusion.4
  430.2 0.9 scatter_custom_fusion.5
  431.0 10.6 %all-reduce.3 = f32[1,32,128]{2,1,0:T(8,128)S(1)} all-reduce(f32[1,32,128]{2,1,0:T(8,128)S(1)} %bitcast.136), channel_id=4, replica_groups=mesh['grp'=2,'scen'=4,'blk'=2,'sub'=2] {'blk','sub'}, use_global_device_ids=true, to_apply=%region_11.12.clone | all-reduce | flops 4096 | bytes 32768
  441.6 0.6 multiply_subtract_fusion.3
  442.2 5.4 all_gather.27
  447.6 0.8 gather_fusion.5
  448.4 79.0 %all-reduce.13.cloned.1.call-done = f32[4096,128]{1,0:T(8,128)} async-done(((f32[4096,128]{1,0:T(8,128)}), f32[4096,128]{1,0:T(8,128)}) %all-reduce.13.cloned.1.call-update) | async-done | bytes 2097168 | tf_op jit(solution)/shard_map/psum | solution.py:136
  527.3 6.2 %multiply_subtract_fusion = (f32[4096,128]{1,0:T(8,128)}, f32[4096,128]{1,0:T(8,128)}) fusion(f32[4096,128]{1,0:T(8,128)} %get-tuple-element.14, f32[4096,128]{1,0:T(8,128)} %all-gather.5.cloned.1.call-done, f32[4096,128]{1,0:T(8,128)} %all-gather.7.cloned.1.call-done, f32[4096,128]{1,0:T(8,128)S(1)} %copy-done.3, f32[4096,128]{1,0:T(8,128)} %all-reduce.13.cloned.1.call-done), kind=kLoop, calls=%fused_computation.24 | loop fusion | flops 3670016 | bytes 14680064 | tf_op jit(solution)/shard_map/sub | solution.py:140
  533.5 2.2 gather_fusion.2
  535.8 8.3 %fusion = f32[64,1,128]{2,1,0:T(1,128)S(1)} fusion(f32[64,128,1]{1,2,0:T(1,128)S(1)} %bitcast.129, f32[1,64,128,128]{3,2,1,0:T(8,128)} %param.15), kind=kOutput, calls=%fused_computation.12 | convolution fusion | flops 12582912 | bytes 4259840 | tf_op jit(solution)/shard_map/skij,skj->ski/dot_general | solution.py:29
  544.1 1.6 multiply_reduce_fusion.2
  545.7 1.6 constant_dynamic-slice_fusion
  547.2 31.1 %all-reduce.4 = (f32[1]{0:T(128)}, f32[1]{0:T(128)}, f32[1]{0:T(128)}) all-reduce(f32[1]{0:T(128)} %bitcast.54, f32[1]{0:T(128)} %bitcast.53, f32[1]{0:T(128)} %bitcast.52), channel_id=1, replica_groups=mesh['grp'=2,'scen'=4,'blk'=2,'sub'=2] {'scen','blk','sub'}, use_global_device_ids=true, to_apply=%region_17.18 | all-reduce | flops 3 | bytes 24 | tf_op jit(solution)/shard_map/psum | solution.py:159
  578.3 2.5 fusion.82
  (50 shorter events, 1.3 us)
Async XLA Ops:
  7.2 28.7 %copy-start = (f32[24,8,128]{2,1,0:T(8,128)S(1)}, f32[24,8,128]{2,1,0:T(8,128)}, u32[]{:S(2)}) copy-start(f32[24,8,128]{2,1,0:T(8,128)} %param.20) | copy-start | bytes 294916
  7.2 110.7 %all-reduce.9.cloned.1.call-start = ((), (), s32[]{:S(2)}) async-start(), calls=%async_computation.4 | async-start | bytes 4194304 | tf_op jit(solution)/shard_map/psum | solution.py:136
  14.8 5.1 copy-start.9
  14.8 6.7 %copy-start.11 = (u32[32]{0:T(128)S(1)}, u32[32]{0:T(128)}, u32[]{:S(2)}) copy-start(u32[32]{0:T(128)} %constant.109) | copy-start | bytes 388
  14.8 21.3 %copy-start.4 = (f32[1,8,128]{2,1,0:T(8,128)S(1)}, f32[1,8,128]{2,1,0:T(8,128)}, u32[]{:S(2)}) copy-start(f32[1,8,128]{2,1,0:T(8,128)} %param.25) | copy-start | bytes 12292
  14.8 21.3 %copy-start.7 = (f32[1,8,128]{2,1,0:T(8,128)S(1)}, f32[1,8,128]{2,1,0:T(8,128)}, u32[]{:S(2)}) copy-start(f32[1,8,128]{2,1,0:T(8,128)} %param.28) | copy-start | bytes 12292
  14.8 21.3 %copy-start.8 = (f32[1,8,128]{2,1,0:T(8,128)S(1)}, f32[1,8,128]{2,1,0:T(8,128)}, u32[]{:S(2)}) copy-start(f32[1,8,128]{2,1,0:T(8,128)} %param.24) | copy-start | bytes 12292
  17.1 143.8 %all-gather.11.cloned.1.call-start = ((), (), s32[]{:S(2)}) async-start(), calls=%async_computation.3 | async-start | bytes 2228224 | tf_op jit(solution)/shard_map/all_gather | solution.py:112
  17.9 185.7 %all-gather.5.cloned.1.call-start = ((), (), s32[]{:S(2)}) async-start(), calls=%async_computation | async-start | bytes 2228224 | tf_op jit(solution)/shard_map/all_gather | solution.py:114
  18.6 227.4 %all-gather.7.cloned.1.call-start = ((), (), s32[]{:S(2)}) async-start(), calls=%async_computation.1 | async-start | bytes 2228224 | tf_op jit(solution)/shard_map/all_gather | solution.py:113
  19.2 269.3 %all-gather.9.cloned.1.call-start = ((), (), s32[]{:S(2)}) async-start(), calls=%async_computation.2 | async-start | bytes 2228224 | tf_op jit(solution)/shard_map/all_gather | solution.py:115
  19.8 386.9 %all-reduce.11.cloned.1.call-start = ((), (), s32[]{:S(2)}) async-start(), calls=%async_computation.5 | async-start | bytes 4194304 | tf_op jit(solution)/shard_map/psum | solution.py:136
  295.0 8.5 %copy-start.6 = (s32[1,64]{1,0:T(1,128)S(1)}, s32[1,64]{1,0:T(1,128)}, u32[]{:S(2)}) copy-start(s32[1,64]{1,0:T(1,128)} %param.16) | copy-start | bytes 772
  295.1 8.5 %copy-start.10 = (f32[1,8,128]{2,1,0:T(8,128)S(1)}, f32[1,8,128]{2,1,0:T(8,128)}, u32[]{:S(2)}) copy-start(f32[1,8,128]{2,1,0:T(8,128)} %param.26) | copy-start | bytes 12292
  295.1 8.8 %copy-start.5 = (f32[1,8,128]{2,1,0:T(8,128)S(1)}, f32[1,8,128]{2,1,0:T(8,128)}, u32[]{:S(2)}) copy-start(f32[1,8,128]{2,1,0:T(8,128)} %param.29) | copy-start | bytes 12292
  295.1 9.0 %copy-start.1 = (f32[1,64,128,128]{3,2,1,0:T(8,128)S(1)}, f32[1,64,128,128]{3,2,1,0:T(8,128)}, u32[]{:S(2)}) copy-start(f32[1,64,128,128]{3,2,1,0:T(8,128)} %param.15) | copy-start | bytes 12582916
  307.7 99.0 %copy-start.3 = (f32[4096,128]{1,0:T(8,128)S(1)}, f32[4096,128]{1,0:T(8,128)}, u32[]{:S(2)}) copy-start(f32[4096,128]{1,0:T(8,128)} %all-gather.11.cloned.1.call-done) | copy-start | bytes 6291460
  310.0 217.3 %all-reduce.13.cloned.1.call-start = ((), (), s32[]{:S(2)}) async-start(), calls=%async_computation.6 | async-start | bytes 4194304 | tf_op jit(solution)/shard_map/psum | solution.py:136
  415.2 9.0 %copy-start.2 = (f32[1,64,128,128]{3,2,1,0:T(8,128)S(1)}, f32[1,64,128,128]{3,2,1,0:T(8,128)}, u32[]{:S(2)}) copy-start(f32[1,64,128,128]{3,2,1,0:T(8,128)} %param.15) | copy-start | bytes 12582916
Sparse Core Ops, SparseCore 0:
  17.2 100.5 all-reduce.8
  120.3 40.6 all-gather.10
  163.3 40.1 all-gather.4
  205.8 40.1 all-gather.6
  248.2 40.1 all-gather.8
  310.2 96.5 all-reduce.10
  430.3 97.0 all-reduce.12
where the time goes:
time: 588 us
  waiting for transfers between devices  407 us (69%)
  blocking collectives  81.2 us (14%)
  matrix products  41.5 us (7%)
  other arithmetic  31.8 us (5%)
  between operations  16.3 us (3%)
  local copies, waits for them, and re-layouts  9.54 us (2%)
    psum x3, waiting for transfers between devices, shards(): grad_first = lax.psum(grad_first_part, ('scen', 'blk', 'sub'))  234 us
    all_gather x1, waiting for transfers between devices, shards(): lax.all_gather(cost_first, ('scen', 'blk', 'sub'), axis=0, tiled=True)  43.1 us
    all_gather x1, waiting for transfers between devices, shards(): lax.all_gather(upper_first, ('scen', 'blk', 'sub'), axis=0, tiled=True)  42.6 us
    all_gather x1, waiting for transfers between devices, shards(): lax.all_gather(lower_first, ('scen', 'blk', 'sub'), axis=0, tiled=True)  42.5 us
    all_gather x1, waiting for transfers between devices, shards(): lax.all_gather(first_start, ('scen', 'blk', 'sub'), axis=0, tiled=True)  42.4 us
    unnamed x3, blocking collectives  34.2 us
    psum x1, blocking collectives, shards(): squares.append(lax.psum(local_square, ('scen', 'blk', 'sub')))  31.1 us
    dot_general x3, matrix products, forward_window(): jnp.einsum('skij,skj->ski', block_matrices, blocks, precision=precise)  25.2 us
  transfers between devices with their start and end apart: 7, of which 7 were waited for; matrix products, arithmetic and copies ran while one was open for 1% of the time, Pallas kernels for 0%

commit v1 on v0

--- a/solution.py
+++ b/solution.py
@@ -133,7 +133,7 @@
         grad_second = lax.psum_scatter(
             grad_second_part, ("blk", "sub"), scatter_dimension=1, tiled=True
         )
-        grad_first = lax.psum(grad_first_part, ("scen", "blk", "sub"))
+        grad_first = lax.psum(lax.psum(grad_first_part, ("blk", "sub")), "scen")
         first_next = jnp.clip(
             first_now - step_primal * (cost_all - grad_first), lower_all, upper_all
         )

time: 588 us -> 677 us (1.15)
  waiting for transfers between devices: 407 us -> 497 us
    psum x3 -> x6, waiting for transfers between devices: 234 us -> 375 us  [shards(): grad_first = lax.psum(lax.psum(grad_first_part, ('blk', 'sub')), 'scen')]
    all_gather x1, waiting for transfers between devices: 43.1 us -> 0.01 us  [shards(): lax.all_gather(cost_first, ('scen', 'blk', 'sub'), axis=0, tiled=True)]
    all_gather x1, waiting for transfers between devices: 42.6 us -> 34.7 us  [shards(): lax.all_gather(upper_first, ('scen', 'blk', 'sub'), axis=0, tiled=True)]
  transfers between devices with their start and end apart: 7 -> 10, of which waited for: 7 -> 9; matrix products, arithmetic and copies ran while one was open for 1% -> 1% of each run, Pallas kernels for 0% -> 0%
where the time goes in v1:
time: 677 us
  waiting for transfers between devices  497 us (73%)
  blocking collectives  78.8 us (12%)
  matrix products  41.5 us (6%)
  other arithmetic  32 us (5%)
  between operations  18 us (3%)
  local copies, waits for them, and re-layouts  9.53 us (1%)
    psum x6, waiting for transfers between devices, shards(): grad_first = lax.psum(lax.psum(grad_first_part, ('blk', 'sub')), 'scen')  375 us
    all_gather x1, waiting for transfers between devices, shards(): lax.all_gather(first_start, ('scen', 'blk', 'sub'), axis=0, tiled=True)  42.3 us
    all_gather x1, waiting for transfers between devices, shards(): lax.all_gather(lower_first, ('scen', 'blk', 'sub'), axis=0, tiled=True)  42.2 us
    all_gather x1, waiting for transfers between devices, shards(): lax.all_gather(upper_first, ('scen', 'blk', 'sub'), axis=0, tiled=True)  34.7 us
    psum x1, blocking collectives, shards(): squares.append(lax.psum(local_square, ('scen', 'blk', 'sub')))  32.1 us
    unnamed x3, blocking collectives  30.9 us
    dot_general x3, matrix products, forward_window(): jnp.einsum('skij,skj->ski', block_matrices, blocks, precision=precise)  25.2 us
    sub x3, other arithmetic, shards(): first_source = 2.0 * first_next - first_now  18.3 us
  transfers between devices with their start and end apart: 10, of which 9 were waited for; matrix products, arithmetic and copies ran while one was open for 1% of the time, Pallas kernels for 0%

profile of v1, /device:TPU:0, one launch (start us, length us, event | category | flops | bytes accessed | tf_op | source)
XLA Modules:
  0.0 676.7 jit_solution(16939191142630857177)
XLA Ops:
  8.7 0.7 fusion.79
  9.4 0.9 fusion.66
  10.3 5.3 fusion.10
  15.6 2.3 scatter_custom_fusion
  18.0 54.2 %all-reduce.12.cloned.1.call-done = f32[4096,128]{1,0:T(8,128)} async-done(((f32[4096,128]{1,0:T(8,128)}), f32[4096,128]{1,0:T(8,128)}) %all-reduce.12.cloned.1.call-update) | async-done | bytes 2097168 | tf_op jit(solution)/shard_map/psum | solution.py:136
  72.3 0.5 all-gather.11.cloned.1.call-update
  72.8 0.5 all-gather.5.cloned.1.call-update
  73.4 0.5 all-gather.7.cloned.1.call-update
  74.0 0.7 all-gather.9.cloned.1.call-update
  74.8 0.9 scatter_custom_fusion.1
  76.3 0.6 dynamic-slice
  77.6 10.5 %all-reduce.1 = f32[1,32,128]{2,1,0:T(8,128)S(1)} all-reduce(f32[1,32,128]{2,1,0:T(8,128)S(1)} %bitcast.135), channel_id=2, replica_groups=mesh['grp'=2,'scen'=4,'blk'=2,'sub'=2] {'blk','sub'}, use_global_device_ids=true, to_apply=%region_4.5.clone | all-reduce | flops 4096 | bytes 32768
  88.3 5.2 all_gather.25
  93.5 0.8 gather_fusion.3
  94.3 77.4 %all-reduce.14.cloned.1.call-done = f32[4096,128]{1,0:T(8,128)} async-done(((f32[4096,128]{1,0:T(8,128)}), f32[4096,128]{1,0:T(8,128)}) %all-reduce.14.cloned.1.call-update) | async-done | bytes 2097168 | tf_op jit(solution)/shard_map/psum | solution.py:136
  171.8 34.7 %all-gather.5.cloned.1.call-done = f32[4096,128]{1,0:T(8,128)} async-done(((f32[256,128]{1,0:T(8,128)}), f32[4096,128]{1,0:T(8,128)}) %all-gather.5.cloned.1.call-update) | async-done | bytes 2097168 | tf_op jit(solution)/shard_map/all_gather | solution.py:114
  206.5 42.2 %all-gather.7.cloned.1.call-done = f32[4096,128]{1,0:T(8,128)} async-done(((f32[256,128]{1,0:T(8,128)}), f32[4096,128]{1,0:T(8,128)}) %all-gather.7.cloned.1.call-update) | async-done | bytes 2097168 | tf_op jit(solution)/shard_map/all_gather | solution.py:113
  248.7 42.3 %all-gather.9.cloned.1.call-done = f32[4096,128]{1,0:T(8,128)} async-done(((f32[256,128]{1,0:T(8,128)}), f32[4096,128]{1,0:T(8,128)}) %all-gather.9.cloned.1.call-update) | async-done | bytes 2097168 | tf_op jit(solution)/shard_map/all_gather | solution.py:115
  291.0 5.9 multiply_subtract_fusion.2
  296.9 0.6 gather_fusion
  297.6 8.5 %fusion.8 = f32[64,1,128]{2,1,0:T(1,128)S(1)} fusion(f32[64,128,1]{1,2,0:T(1,128)S(1)} %bitcast.130, f32[1,64,128,128]{3,2,1,0:T(8,128)} %param.15), kind=kOutput, calls=%fused_computation.20 | convolution fusion | flops 12582912 | bytes 4259840 | tf_op jit(solution)/shard_map/skij,skj->ski/dot_general | solution.py:29
  306.6 3.7 fusion.6
  310.3 2.4 scatter_custom_fusion.2
  312.7 50.0 %all-reduce.16.cloned.1.call-done = f32[4096,128]{1,0:T(8,128)} async-done(((f32[4096,128]{1,0:T(8,128)}), f32[4096,128]{1,0:T(8,128)}) %all-reduce.16.cloned.1.call-update) | async-done | bytes 2097168 | tf_op jit(solution)/shard_map/psum | solution.py:136
  362.8 0.9 scatter_custom_fusion.3
  363.7 10.3 %all-reduce.2 = f32[1,32,128]{2,1,0:T(8,128)S(1)} all-reduce(f32[1,32,128]{2,1,0:T(8,128)S(1)} %bitcast.137), channel_id=3, replica_groups=mesh['grp'=2,'scen'=4,'blk'=2,'sub'=2] {'blk','sub'}, use_global_device_ids=true, to_apply=%region_9.10.clone | all-reduce | flops 4096 | bytes 32768
  374.0 5.2 all_gather.26
  379.2 0.8 gather_fusion.4
  380.0 71.7 %all-reduce.18.cloned.1.call-done = f32[4096,128]{1,0:T(8,128)} async-done(((f32[4096,128]{1,0:T(8,128)}), f32[4096,128]{1,0:T(8,128)}) %all-reduce.18.cloned.1.call-update) | async-done | bytes 2097168 | tf_op jit(solution)/shard_map/psum | solution.py:136
  451.7 6.2 multiply_subtract_fusion.1
  457.9 2.2 gather_fusion.1
  460.2 8.5 %fusion.4 = f32[64,1,128]{2,1,0:T(1,128)S(1)} fusion(f32[64,128,1]{1,2,0:T(1,128)S(1)} %bitcast.131, f32[1,64,128,128]{3,2,1,0:T(8,128)} %param.15), kind=kOutput, calls=%fused_computation.16 | convolution fusion | flops 12582912 | bytes 4259840 | tf_op jit(solution)/shard_map/skij,skj->ski/dot_general | solution.py:29
  469.1 3.7 fusion.2
  472.8 2.4 scatter_custom_fusion.4
  475.2 50.4 %all-reduce.20.cloned.1.call-done = f32[4096,128]{1,0:T(8,128)} async-done(((f32[4096,128]{1,0:T(8,128)}), f32[4096,128]{1,0:T(8,128)}) %all-reduce.20.cloned.1.call-update) | async-done | bytes 2097168 | tf_op jit(solution)/shard_map/psum | solution.py:136
  525.7 0.9 scatter_custom_fusion.5
  526.6 10.1 %all-reduce.3 = f32[1,32,128]{2,1,0:T(8,128)S(1)} all-reduce(f32[1,32,128]{2,1,0:T(8,128)S(1)} %bitcast.136), channel_id=4, replica_groups=mesh['grp'=2,'scen'=4,'blk'=2,'sub'=2] {'blk','sub'}, use_global_device_ids=true, to_apply=%region_14.15.clone | all-reduce | flops 4096 | bytes 32768
  536.7 0.6 multiply_subtract_fusion.3
  537.3 5.4 all_gather.27
  542.7 0.8 gather_fusion.5
  543.5 71.2 %all-reduce.22.cloned.1.call-done = f32[4096,128]{1,0:T(8,128)} async-done(((f32[4096,128]{1,0:T(8,128)}), f32[4096,128]{1,0:T(8,128)}) %all-reduce.22.cloned.1.call-update) | async-done | bytes 2097168 | tf_op jit(solution)/shard_map/psum | solution.py:136
  614.6 6.2 multiply_subtract_fusion
  620.8 2.2 gather_fusion.2
  623.1 8.3 %fusion = f32[64,1,128]{2,1,0:T(1,128)S(1)} fusion(f32[64,128,1]{1,2,0:T(1,128)S(1)} %bitcast.129, f32[1,64,128,128]{3,2,1,0:T(8,128)} %param.15), kind=kOutput, calls=%fused_computation.12 | convolution fusion | flops 12582912 | bytes 4259840 | tf_op jit(solution)/shard_map/skij,skj->ski/dot_general | solution.py:29
  631.4 1.6 multiply_reduce_fusion.2
  633.0 1.6 constant_dynamic-slice_fusion
  634.5 32.1 %all-reduce.4 = (f32[1]{0:T(128)}, f32[1]{0:T(128)}, f32[1]{0:T(128)}) all-reduce(f32[1]{0:T(128)} %bitcast.54, f32[1]{0:T(128)} %bitcast.53, f32[1]{0:T(128)} %bitcast.52), channel_id=1, replica_groups=mesh['grp'=2,'scen'=4,'blk'=2,'sub'=2] {'scen','blk','sub'}, use_global_device_ids=true, to_apply=%region_20.21 | all-reduce | flops 3 | bytes 24 | tf_op jit(solution)/shard_map/psum | solution.py:159
  666.6 2.5 fusion.82
  (59 shorter events, 2.0 us)
Async XLA Ops:
  8.0 80.1 %copy-start = (f32[24,8,128]{2,1,0:T(8,128)S(1)}, f32[24,8,128]{2,1,0:T(8,128)}, u32[]{:S(2)}) copy-start(f32[24,8,128]{2,1,0:T(8,128)} %param.20) | copy-start | bytes 294916
  8.0 64.2 %all-reduce.12.cloned.1.call-start = ((), (), s32[]{:S(2)}) async-start(), calls=%async_computation.4 | async-start | bytes 4194304 | tf_op jit(solution)/shard_map/psum | solution.py:136
  17.9 56.8 %copy-start.9 = (s32[1,64]{1,0:T(1,128)S(1)}, s32[1,64]{1,0:T(1,128)}, u32[]{:S(2)}) copy-start(s32[1,64]{1,0:T(1,128)} %param.17) | copy-start | bytes 772
  17.9 58.4 %copy-start.11 = (u32[32]{0:T(128)S(1)}, u32[32]{0:T(128)}, u32[]{:S(2)}) copy-start(u32[32]{0:T(128)} %constant.109) | copy-start | bytes 388
  17.9 70.4 %copy-start.4 = (f32[1,8,128]{2,1,0:T(8,128)S(1)}, f32[1,8,128]{2,1,0:T(8,128)}, u32[]{:S(2)}) copy-start(f32[1,8,128]{2,1,0:T(8,128)} %param.25) | copy-start | bytes 12292
  17.9 70.4 %copy-start.7 = (f32[1,8,128]{2,1,0:T(8,128)S(1)}, f32[1,8,128]{2,1,0:T(8,128)}, u32[]{:S(2)}) copy-start(f32[1,8,128]{2,1,0:T(8,128)} %param.28) | copy-start | bytes 12292
  17.9 70.4 %copy-start.8 = (f32[1,8,128]{2,1,0:T(8,128)S(1)}, f32[1,8,128]{2,1,0:T(8,128)}, u32[]{:S(2)}) copy-start(f32[1,8,128]{2,1,0:T(8,128)} %param.24) | copy-start | bytes 12292
  18.0 153.8 %all-reduce.14.cloned.1.call-start = ((), (), s32[]{:S(2)}) async-start(), calls=%async_computation.5 | async-start | bytes 4194304 | tf_op jit(solution)/shard_map/psum | solution.py:136
  72.2 99.6 %all-gather.11.cloned.1.call-start = ((), (), s32[]{:S(2)}) async-start(), calls=%async_computation.3 | async-start | bytes 2228224 | tf_op jit(solution)/shard_map/all_gather | solution.py:112
  72.8 133.7 %all-gather.5.cloned.1.call-start = ((), (), s32[]{:S(2)}) async-start(), calls=%async_computation | async-start | bytes 2228224 | tf_op jit(solution)/shard_map/all_gather | solution.py:114
  73.4 175.3 %all-gather.7.cloned.1.call-start = ((), (), s32[]{:S(2)}) async-start(), calls=%async_computation.1 | async-start | bytes 2228224 | tf_op jit(solution)/shard_map/all_gather | solution.py:113
  74.0 217.0 %all-gather.9.cloned.1.call-start = ((), (), s32[]{:S(2)}) async-start(), calls=%async_computation.2 | async-start | bytes 2228224 | tf_op jit(solution)/shard_map/all_gather | solution.py:115
  74.7 288.0 %all-reduce.16.cloned.1.call-start = ((), (), s32[]{:S(2)}) async-start(), calls=%async_computation.6 | async-start | bytes 4194304 | tf_op jit(solution)/shard_map/psum | solution.py:136
  297.6 8.5 %copy-start.6 = (s32[1,64]{1,0:T(1,128)S(1)}, s32[1,64]{1,0:T(1,128)}, u32[]{:S(2)}) copy-start(s32[1,64]{1,0:T(1,128)} %param.16) | copy-start | bytes 772
  297.6 8.5 %copy-start.10 = (f32[1,8,128]{2,1,0:T(8,128)S(1)}, f32[1,8,128]{2,1,0:T(8,128)}, u32[]{:S(2)}) copy-start(f32[1,8,128]{2,1,0:T(8,128)} %param.26) | copy-start | bytes 12292
  297.6 8.8 %copy-start.5 = (f32[1,8,128]{2,1,0:T(8,128)S(1)}, f32[1,8,128]{2,1,0:T(8,128)}, u32[]{:S(2)}) copy-start(f32[1,8,128]{2,1,0:T(8,128)} %param.29) | copy-start | bytes 12292
  297.6 9.0 %copy-start.1 = (f32[1,64,128,128]{3,2,1,0:T(8,128)S(1)}, f32[1,64,128,128]{3,2,1,0:T(8,128)}, u32[]{:S(2)}) copy-start(f32[1,64,128,128]{3,2,1,0:T(8,128)} %param.15) | copy-start | bytes 12582916
  312.6 139.1 %copy-start.3 = (f32[4096,128]{1,0:T(8,128)S(1)}, f32[4096,128]{1,0:T(8,128)}, u32[]{:S(2)}) copy-start(f32[4096,128]{1,0:T(8,128)} %all-gather.11.cloned.1.call-done) | copy-start | bytes 6291460
  312.7 139.0 %all-reduce.18.cloned.1.call-start = ((), (), s32[]{:S(2)}) async-start(), calls=%async_computation.7 | async-start | bytes 4194304 | tf_op jit(solution)/shard_map/psum | solution.py:136
  362.8 162.9 %all-reduce.20.cloned.1.call-start = ((), (), s32[]{:S(2)}) async-start(), calls=%async_computation.8 | async-start | bytes 4194304 | tf_op jit(solution)/shard_map/psum | solution.py:136
  460.1 9.0 %copy-start.2 = (f32[1,64,128,128]{3,2,1,0:T(8,128)S(1)}, f32[1,64,128,128]{3,2,1,0:T(8,128)}, u32[]{:S(2)}) copy-start(f32[1,64,128,128]{3,2,1,0:T(8,128)} %param.15) | copy-start | bytes 12582916
  475.2 139.4 %all-reduce.22.cloned.1.call-start = ((), (), s32[]{:S(2)}) async-start(), calls=%async_computation.9 | async-start | bytes 4194304 | tf_op jit(solution)/shard_map/psum | solution.py:136
Sparse Core Ops, SparseCore 0:
  18.1 54.0 all-reduce.11
  74.7 97.0 all-reduce.13
  312.8 49.9 all-reduce.15
  365.1 86.5 all-reduce.17
  475.3 50.3 all-reduce.19
  528.0 86.5 all-reduce.21
Sparse Core Ops, SparseCore 1:
  74.8 88.6 all-gather.10
  165.5 40.9 all-gather.4
  208.5 40.1 all-gather.6
  250.9 40.1 all-gather.8
